TPU v7x, 512 devices: a whole 4x4x16 slice. The times are simulated.
512 devices in a mesh: row: 8 (over y, core), col: 8 (over z_lo), depth: 8 (over z_hi, x).
Axes of the slice: x: 4, y: 4, z: 16 (z_hi: 2, z_lo: 8; z = z_hi * 8 + z_lo), core: 2. Of those that a mesh axis runs over, the one named last changes fastest.
Arguments:
- tokens: bfloat16 [1024, 4096], P(('col', 'depth'), 'row'), may hold values from -6 to 6
- out_grad: bfloat16 [1024, 4096], P(('col', 'depth'), 'row'), may hold values from -2 to 2
- w_in: bfloat16 [4096, 14336], P('row', 'col'), may hold values from -0.09375 to 0.09375
- b_in: float32 [14336], P('col'), may hold values from -3 to 3
- w_out: bfloat16 [14336, 4096], P('col', 'row'), may hold values from -0.046875 to 0.046875
Outputs:
- block_out: bfloat16 [1024, 4096], P(('col', 'depth'), 'row')
- tokens_grad: bfloat16 [1024, 4096], P(('col', 'depth'), 'row')
- w_in_grad: bfloat16 [4096, 14336], P('row', ('col', 'depth'))
- w_out_grad: bfloat16 [14336, 4096], P(('col', 'depth'), 'row')
- b_in_grad: float32 [14336], P('col')
All inputs are finite; a program needn't handle non-finite values.
Results may differ from a plain program's by a relative error of at most 0.005.
Values may be sent and summed in bfloat16 or wider, within the bound.
No kernel may reach another device: no remote copies, remote signals or barrier semaphores. Data moves between devices by JAX's collectives and lax.ppermute only.
A program may use at most 64 MiB of HBM per device.

v0:
```python
import jax
import jax.numpy as jnp
from jax import lax
from jax.sharding import PartitionSpec as P

root_coeff = 0.7978845608028654
cubic_coeff = 0.044715


def gelu_parts(pre_act):
    inner_arg = root_coeff * (pre_act + cubic_coeff * pre_act * pre_act * pre_act)
    tangent = jnp.tanh(inner_arg)
    gelu_value = 0.5 * pre_act * (1.0 + tangent)
    gelu_slope = 0.5 * (1.0 + tangent) + 0.5 * pre_act * (1.0 - tangent * tangent) * root_coeff * (
        1.0 + 3.0 * cubic_coeff * pre_act * pre_act
    )
    return (gelu_value, gelu_slope)


def right_transposed(left_side, right_side):
    return lax.dot_general(
        left_side, right_side, (((1,), (1,)), ((), ())), preferred_element_type=jnp.float32
    )


def left_transposed(left_side, right_side):
    return lax.dot_general(
        left_side, right_side, (((0,), (0,)), ((), ())), preferred_element_type=jnp.float32
    )


def depth_rows(gathered, col_count, depth_index, depth_count):
    tile_rows = gathered.shape[0] // (col_count * depth_count)
    shaped = gathered.reshape(col_count, depth_count, tile_rows, gathered.shape[1])
    picked = lax.dynamic_index_in_dim(shaped, depth_index, 1, keepdims=False)
    return picked.reshape(col_count * tile_rows, gathered.shape[1])


def local(tokens, out_grad, w_in, b_in, w_out):
    col_count = lax.axis_size("col")
    depth_count = lax.axis_size("depth")
    tile_rows = tokens.shape[0]
    part_cols = w_in.shape[1] // depth_count
    depth_index = lax.axis_index("depth")
    all_input, all_grad = (
        lax.all_gather(tokens, ("col", "depth"), axis=0, tiled=True),
        lax.all_gather(out_grad, ("col", "depth"), axis=0, tiled=True),
    )
    plane_input = depth_rows(all_input, col_count, depth_index, depth_count)
    plane_grad = depth_rows(all_grad, col_count, depth_index, depth_count)
    pre_sum = lax.psum_scatter(
        jnp.dot(plane_input, w_in, preferred_element_type=jnp.float32),
        "row",
        scatter_dimension=0,
        tiled=True,
    )
    pre_share = pre_sum + b_in
    gelu_value, gelu_slope = gelu_parts(pre_share)
    plane_act = lax.all_gather(gelu_value.astype(jnp.bfloat16), "row", axis=0, tiled=True)
    block_out = lax.psum_scatter(
        jnp.dot(plane_act, w_out, preferred_element_type=jnp.float32),
        "col",
        scatter_dimension=0,
        tiled=True,
    ).astype(jnp.bfloat16)
    grad_share = lax.psum_scatter(
        right_transposed(plane_grad, w_out), "row", scatter_dimension=0, tiled=True
    )
    pre_grad = grad_share * gelu_slope
    plane_hgrad = lax.all_gather(pre_grad.astype(jnp.bfloat16), "row", axis=0, tiled=True)
    b_in_grad = lax.psum(jnp.sum(pre_grad, axis=0), ("row", "depth"))
    tokens_grad = lax.psum_scatter(
        right_transposed(plane_hgrad, w_in), "col", scatter_dimension=0, tiled=True
    ).astype(jnp.bfloat16)
    act_parts = lax.all_to_all(
        plane_act.reshape(col_count, tile_rows, w_in.shape[1]),
        "depth",
        split_axis=2,
        concat_axis=1,
        tiled=True,
    )
    act_parts = act_parts.reshape(-1, part_cols)
    hgrad_parts = lax.all_to_all(
        plane_hgrad.reshape(col_count, tile_rows, w_in.shape[1]),
        "depth",
        split_axis=2,
        concat_axis=1,
        tiled=True,
    )
    hgrad_parts = hgrad_parts.reshape(-1, part_cols)
    w_in_grad = left_transposed(all_input, hgrad_parts)
    w_out_grad = left_transposed(act_parts, all_grad)
    return (
        block_out,
        tokens_grad,
        w_in_grad.astype(jnp.bfloat16),
        w_out_grad.astype(jnp.bfloat16),
        b_in_grad,
    )


def solution(mesh):
    return jax.shard_map(
        local,
        mesh=mesh,
        in_specs=(
            P(("col", "depth"), "row"),
            P(("col", "depth"), "row"),
            P("row", "col"),
            P("col"),
            P("col", "row"),
        ),
        out_specs=(
            P(("col", "depth"), "row"),
            P(("col", "depth"), "row"),
            P("row", ("col", "depth")),
            P(("col", "depth"), "row"),
            P("col"),
        ),
        check_vma=False,
    )
```

profile of v0, /device:TPU:32, one launch (start us, length us, event | category | flops | bytes accessed | tf_op | source)
XLA Modules:
  0.0 1477.0 jit_solution(16970488687303766909)
XLA Ops:
  8.7 482.7 %all-gather.3.cloned.1.call-done = bf16[1024,512]{1,0:T(8,128)(2,1)} async-done(((bf16[16,512]{1,0:T(8,128)(2,1)}), bf16[1024,512]{1,0:T(8,128)(2,1)}) %all-gather.3.cloned.1.call-update) | async-done | bytes 1048592 | tf_op jit(solution)/shard_map/all_gather | solution.py:46
  491.4 488.3 %all-gather.5.cloned.1.call-done = bf16[1024,512]{1,0:T(8,128)(2,1)} async-done(((bf16[16,512]{1,0:T(8,128)(2,1)}), bf16[1024,512]{1,0:T(8,128)(2,1)}) %all-gather.5.cloned.1.call-update) | async-done | bytes 1048592 | tf_op jit(solution)/shard_map/all_gather | solution.py:47
  982.2 3.2 fusion.11
  985.4 45.7 %reduce-scatter.5.cloned.1.call-done = f32[16,1792]{1,0:T(8,128)} async-done(((f32[128,1792]{1,0:T(8,128)}), f32[16,1792]{1,0:T(8,128)}) %reduce-scatter.5.cloned.1.call-update) | async-done | bytes 114704 | tf_op jit(solution)/shard_map/reduce_scatter | solution.py:51
  1031.2 41.2 %reduce-scatter.9.cloned.1.call-done = f32[16,1792]{1,0:T(8,128)} async-done(((f32[128,1792]{1,0:T(8,128)}), f32[16,1792]{1,0:T(8,128)}) %reduce-scatter.9.cloned.1.call-update) | async-done | bytes 114704 | tf_op jit(solution)/shard_map/reduce_scatter | solution.py:66
  1073.5 13.0 all_gather.13
  1086.5 3.7 copy.15
  1090.2 6.0 reshape.49
  1096.2 13.8 all-to-all-start.1
  1109.9 13.0 all_gather.15
  1123.0 3.7 copy.12
  1126.6 5.9 reshape.47
  1132.6 9.8 all-to-all-done.1
  1142.4 4.7 all-to-all-start
  1147.1 1.4 fusion.12
  1148.6 2.6 fusion.10
  1151.2 295.6 %psum.7 = f32[1792]{0:T(1024)} all-reduce(f32[1792]{0:T(1024)S(1)} %get-tuple-element.5), channel_id=1, replica_groups=mesh['row'=8,'col'=8,'depth'=8] {'row','depth'}, use_global_device_ids=true, to_apply=%region_5.6 | all-reduce | flops 1792 | bytes 14336 | tf_op jit(solution)/shard_map/psum | solution.py:71
  1446.8 1.4 convert_element_type.24
  1448.2 1.4 convert_element_type.22
  1449.6 3.9 reshape.50
  1453.4 4.1 copy.17
  1457.5 5.1 reshape.48
  1462.6 4.1 copy.14
  1466.6 2.4 convolution_convert_fusion
  (25 shorter events, 6.2 us)
Async XLA Ops:
  7.2 973.6 %copy-start = (bf16[512,1792]{1,0:T(8,128)(2,1)S(1)}, bf16[512,1792]{1,0:T(8,128)(2,1)}, u32[]{:S(2)}) copy-start(bf16[512,1792]{1,0:T(8,128)(2,1)} %param.7) | copy-start | bytes 5505028
  7.2 484.3 %all-gather.3.cloned.1.call-start = ((), (), s32[]{:S(2)}) async-start(), calls=%async_computation.6 | async-start | bytes 1064960 | tf_op jit(solution)/shard_map/all_gather | solution.py:46
  7.9 971.9 %all-gather.5.cloned.1.call-start = ((), (), s32[]{:S(2)}) async-start(), calls=%async_computation.9 | async-start | bytes 1064960 | tf_op jit(solution)/shard_map/all_gather | solution.py:47
  8.7 1022.5 %reduce-scatter.5.cloned.1.call-start = ((), (), s32[]{:S(2)}) async-start(), calls=%async_computation.7 | async-start | bytes 1032192 | tf_op jit(solution)/shard_map/reduce_scatter | solution.py:51
  982.2 90.2 %reduce-scatter.9.cloned.1.call-start = ((), (), s32[]{:S(2)}) async-start(), calls=%async_computation.10 | async-start | bytes 1032192 | tf_op jit(solution)/shard_map/reduce_scatter | solution.py:66
  982.2 90.2 %copy-start.2 = (f32[1792]{0:T(1024)S(1)}, f32[1792]{0:T(1024)}, u32[]{:S(2)}) copy-start(f32[1792]{0:T(1024)} %param.8) | copy-start | bytes 21508
  1096.2 46.2 %all-to-all-start.1 = ((bf16[8,2,14336]{2,1,0:T(2,128)(2,1)}), bf16[8,2,14336]{2,1,0:T(2,128)(2,1)S(1)}, u32[]{:S(2)}, u32[]{:S(2)}) async-start(bf16[8,2,14336]{2,1,0:T(2,128)(2,1)} %reshape.49), calls=%async_computation.5 | async-start | bytes 917504 | tf_op jit(solution)/shard_map/all_to_all | solution.py:75
  1142.4 315.1 %all-to-all-start = ((bf16[8,2,14336]{2,1,0:T(2,128)(2,1)}), bf16[8,2,14336]{2,1,0:T(2,128)(2,1)}, u32[]{:S(2)}, u32[]{:S(2)}) async-start(bf16[8,2,14336]{2,1,0:T(2,128)(2,1)} %reshape.47), calls=%async_computation.4 | async-start | bytes 917504 | tf_op jit(solution)/shard_map/all_to_all | solution.py:83
  1147.0 299.8 %reduce-scatter.11.cloned.1.call-start = ((), (), s32[]{:S(2)}) async-start(), calls=%async_computation.11 | async-start | bytes 294912 | tf_op jit(solution)/shard_map/reduce_scatter | solution.py:72
  1148.5 299.7 %reduce-scatter.7.cloned.1.call-start = ((), (), s32[]{:S(2)}) async-start(), calls=%async_computation.8 | async-start | bytes 294912 | tf_op jit(solution)/shard_map/reduce_scatter | solution.py:60
  1466.6 2.4 copy-start.1
Sparse Core Ops, SparseCore 0:
  10.1 481.3 all-gather.2
  493.5 486.2 all-gather.4
  982.6 48.5 reduce-scatter.4
  1033.9 38.4 reduce-scatter.8
  1150.3 59.0 reduce-scatter.10
  1212.1 56.2 reduce-scatter.6
where the time goes:
time: 1480 us
  waiting for transfers between devices  1070 us (72%)
  blocking collectives  322 us (22%)
  local copies, waits for them, and re-layouts  37.3 us (3%)
  starting transfers between devices  18.7 us (1%)
    all_gather x1, waiting for transfers between devices, local(): lax.all_gather(out_grad, ('col', 'depth'), axis=0, tiled=True)  488 us
    all_gather x1, waiting for transfers between devices, local(): lax.all_gather(tokens, ('col', 'depth'), axis=0, tiled=True)  483 us
    psum x1, blocking collectives, local(): b_in_grad = lax.psum(jnp.sum(pre_grad, axis=0), ('row', 'depth'))  296 us
    reduce_scatter x1, waiting for transfers between devices, local(): lax.psum_scatter(jnp.dot(plane_input, w_in, preferred_element_type=jnp.fl...  45.7 us
    reduce_scatter x1, waiting for transfers between devices, local(): lax.psum_scatter(right_transposed(plane_grad, w_out), 'row', scatter_dime...  41.2 us
  transfers between devices with their start and end apart: 8, of which 5 were waited for; matrix products, arithmetic and copies ran while one was open for 2% of the time, Pallas kernels for 0%

commit v1 on v0

--- a/solution.py
+++ b/solution.py
@@ -43,7 +43,12 @@
     part_cols = w_in.shape[1] // depth_count
     depth_index = lax.axis_index("depth")
     all_input, all_grad = (
-        lax.all_gather(tokens, ("col", "depth"), axis=0, tiled=True),
+        jnp.concatenate(
+            lax.all_to_all(
+                jnp.stack([tokens] * lax.axis_size(("col", "depth"))), ("col", "depth"), 0, 0
+            ),
+            axis=0,
+        ),
         lax.all_gather(out_grad, ("col", "depth"), axis=0, tiled=True),
     )
     plane_input = depth_rows(all_input, col_count, depth_index, depth_count)

time: 1480 us -> 1010 us (0.68)
  waiting for transfers between devices: 1070 us -> 580 us
  starting transfers between devices: 18.7 us -> 36.7 us
    all_gather x1 -> x0, waiting for transfers between devices: 483 us -> none  [local(): lax.all_gather(tokens, ('col', 'depth'), axis=0, tiled=True)]
    all_to_all x0 -> x1, starting transfers between devices: none -> 18.2 us  [local(): lax.all_to_all(jnp.stack([tokens] * lax.axis_size(('col', 'depth'))), ('c...]
  transfers between devices with their start and end apart: 8 -> 8, of which waited for: 5 -> 4; matrix products, arithmetic and copies ran while one was open for 2% -> 3% of each run, Pallas kernels for 0% -> 0%
where the time goes in v1:
time: 1010 us
  waiting for transfers between devices  580 us (57%)
  blocking collectives  322 us (32%)
  local copies, waits for them, and re-layouts  40.1 us (4%)
  starting transfers between devices  36.7 us (4%)
  between operations  13.9 us (1%)
  matrix products  12 us (1%)
    all_gather x1, waiting for transfers between devices, local(): lax.all_gather(out_grad, ('col', 'depth'), axis=0, tiled=True)  483 us
    psum x1, blocking collectives, local(): b_in_grad = lax.psum(jnp.sum(pre_grad, axis=0), ('row', 'depth'))  296 us
    reduce_scatter x1, waiting for transfers between devices, local(): lax.psum_scatter(jnp.dot(plane_input, w_in, preferred_element_type=jnp.fl...  45.1 us
    reduce_scatter x1, waiting for transfers between devices, local(): lax.psum_scatter(right_transposed(plane_grad, w_out), 'row', scatter_dime...  41.4 us
    unnamed x14, local copies, waits for them, and re-layouts  20.9 us
  transfers between devices with their start and end apart: 8, of which 4 were waited for; matrix products, arithmetic and copies ran while one was open for 3% of the time, Pallas kernels for 0%

profile of v1, /device:TPU:32, one launch (start us, length us, event | category | flops | bytes accessed | tf_op | source)
XLA Modules:
  0.0 1007.7 jit_solution(3870342761068955431)
XLA Ops:
  7.2 2.0 stack.2
  9.1 18.2 %all-to-all-start = ((bf16[64,16,512]{2,1,0:T(8,128)(2,1)}), bf16[64,16,512]{2,1,0:T(8,128)(2,1)S(1)}, u32[]{:S(2)}, u32[]{:S(2)}) async-start(bf16[64,16,512]{2,1,0:T(8,128)(2,1)} %stack.2), calls=%async_computation | async-start | bytes 2097152 | tf_op jit(solution)/shard_map/all_to_all | solution.py:47
  28.1 482.7 %all-gather.2.cloned.1.call-done = bf16[1024,512]{1,0:T(8,128)(2,1)} async-done(((bf16[16,512]{1,0:T(8,128)(2,1)}), bf16[1024,512]{1,0:T(8,128)(2,1)}) %all-gather.2.cloned.1.call-update) | async-done | bytes 1048592 | tf_op jit(solution)/shard_map/all_gather | solution.py:52
  513.3 3.2 fusion.11
  516.5 45.1 %reduce-scatter.5.cloned.1.call-done = f32[16,1792]{1,0:T(8,128)} async-done(((f32[128,1792]{1,0:T(8,128)}), f32[16,1792]{1,0:T(8,128)}) %reduce-scatter.5.cloned.1.call-update) | async-done | bytes 114704 | tf_op jit(solution)/shard_map/reduce_scatter | solution.py:56
  561.6 41.4 %reduce-scatter.9.cloned.1.call-done = f32[16,1792]{1,0:T(8,128)} async-done(((f32[128,1792]{1,0:T(8,128)}), f32[16,1792]{1,0:T(8,128)}) %reduce-scatter.9.cloned.1.call-update) | async-done | bytes 114704 | tf_op jit(solution)/shard_map/reduce_scatter | solution.py:71
  604.1 13.0 %all_gather.9 = bf16[128,1792]{1,0:T(8,128)(2,1)S(1)} all-gather(bf16[16,1792]{1,0:T(8,128)(2,1)S(1)} %get-tuple-element.7), channel_id=1, replica_groups=mesh['row'=8,'col'=8,'depth'=8] {'row'}, dimensions={0}, use_global_device_ids=true | all-gather | bytes 516096 | tf_op jit(solution)/shard_map/all_gather | solution.py:64
  617.1 3.7 copy.15
  620.8 5.9 reshape.51
  626.8 13.6 %all-to-all-start.2 = ((bf16[8,2,14336]{2,1,0:T(2,128)(2,1)}), bf16[8,2,14336]{2,1,0:T(2,128)(2,1)S(1)}, u32[]{:S(2)}, u32[]{:S(2)}) async-start(bf16[8,2,14336]{2,1,0:T(2,128)(2,1)} %reshape.51), calls=%async_computation.6 | async-start | bytes 917504 | tf_op jit(solution)/shard_map/all_to_all | solution.py:80
  640.4 13.0 %all_gather.11 = bf16[128,1792]{1,0:T(8,128)(2,1)S(1)} all-gather(bf16[16,1792]{1,0:T(8,128)(2,1)S(1)} %get-tuple-element.6), channel_id=1, replica_groups=mesh['row'=8,'col'=8,'depth'=8] {'row'}, dimensions={0}, use_global_device_ids=true | all-gather | bytes 516096 | tf_op jit(solution)/shard_map/all_gather | solution.py:75
  653.4 3.7 copy.12
  657.1 5.9 reshape.49
  663.1 9.8 all-to-all-done.2
  672.9 4.6 all-to-all-start.1
  677.5 1.4 fusion.12
  679.0 2.6 fusion.10
  681.7 295.6 %psum.7 = f32[1792]{0:T(1024)} all-reduce(f32[1792]{0:T(1024)S(1)} %get-tuple-element.5), channel_id=1, replica_groups=mesh['row'=8,'col'=8,'depth'=8] {'row','depth'}, use_global_device_ids=true, to_apply=%region_5.6 | all-reduce | flops 1792 | bytes 14336 | tf_op jit(solution)/shard_map/psum | solution.py:76
  977.3 1.4 convert_element_type.24
  980.0 3.9 reshape.52
  983.9 4.1 copy.17
  987.9 5.1 reshape.50
  993.0 4.8 copy.14
  997.8 2.2 fusion
  (29 shorter events, 6.9 us)
Async XLA Ops:
  7.2 504.7 %copy-start = (bf16[512,1792]{1,0:T(8,128)(2,1)S(1)}, bf16[512,1792]{1,0:T(8,128)(2,1)}, u32[]{:S(2)}) copy-start(bf16[512,1792]{1,0:T(8,128)(2,1)} %param.7) | copy-start | bytes 5505028
  9.1 501.7 %all-to-all-start = ((bf16[64,16,512]{2,1,0:T(8,128)(2,1)}), bf16[64,16,512]{2,1,0:T(8,128)(2,1)S(1)}, u32[]{:S(2)}, u32[]{:S(2)}) async-start(bf16[64,16,512]{2,1,0:T(8,128)(2,1)} %stack.2), calls=%async_computation | async-start | bytes 2097152 | tf_op jit(solution)/shard_map/all_to_all | solution.py:47
  27.4 483.4 %all-gather.2.cloned.1.call-start = ((), (), s32[]{:S(2)}) async-start(), calls=%async_computation.9 | async-start | bytes 1064960 | tf_op jit(solution)/shard_map/all_gather | solution.py:52
  28.1 533.5 %reduce-scatter.5.cloned.1.call-start = ((), (), s32[]{:S(2)}) async-start(), calls=%async_computation.7 | async-start | bytes 1032192 | tf_op jit(solution)/shard_map/reduce_scatter | solution.py:56
  510.8 2.4 copy-start.1
  513.2 89.8 %reduce-scatter.9.cloned.1.call-start = ((), (), s32[]{:S(2)}) async-start(), calls=%async_computation.10 | async-start | bytes 1032192 | tf_op jit(solution)/shard_map/reduce_scatter | solution.py:71
  513.3 89.7 %copy-start.4 = (f32[1792]{0:T(1024)S(1)}, f32[1792]{0:T(1024)}, u32[]{:S(2)}) copy-start(f32[1792]{0:T(1024)} %param.8) | copy-start | bytes 21508
  626.8 46.1 %all-to-all-start.2 = ((bf16[8,2,14336]{2,1,0:T(2,128)(2,1)}), bf16[8,2,14336]{2,1,0:T(2,128)(2,1)S(1)}, u32[]{:S(2)}, u32[]{:S(2)}) async-start(bf16[8,2,14336]{2,1,0:T(2,128)(2,1)} %reshape.51), calls=%async_computation.6 | async-start | bytes 917504 | tf_op jit(solution)/shard_map/all_to_all | solution.py:80
  672.9 315.1 %all-to-all-start.1 = ((bf16[8,2,14336]{2,1,0:T(2,128)(2,1)}), bf16[8,2,14336]{2,1,0:T(2,128)(2,1)}, u32[]{:S(2)}, u32[]{:S(2)}) async-start(bf16[8,2,14336]{2,1,0:T(2,128)(2,1)} %reshape.49), calls=%async_computation.5 | async-start | bytes 917504 | tf_op jit(solution)/shard_map/all_to_all | solution.py:88
  677.5 299.8 %reduce-scatter.11.cloned.1.call-start = ((), (), s32[]{:S(2)}) async-start(), calls=%async_computation.11 | async-start | bytes 294912 | tf_op jit(solution)/shard_map/reduce_scatter | solution.py:77
  679.0 299.6 %reduce-scatter.7.cloned.1.call-start = ((), (), s32[]{:S(2)}) async-start(), calls=%async_computation.8 | async-start | bytes 294912 | tf_op jit(solution)/shard_map/reduce_scatter | solution.py:65
  993.0 4.8 copy-start.2
  997.8 2.2 copy-start.3
Sparse Core Ops, SparseCore 0:
  30.2 480.5 all-gather.1
  513.6 47.9 reduce-scatter.4
  564.4 38.5 reduce-scatter.8
  680.8 59.1 reduce-scatter.10
  742.6 56.2 reduce-scatter.6
